TPU v7x, 32 devices: a whole 2x2x4 slice. The times are simulated.
32 devices in a mesh: head: 2 (over y), ctx: 16 (over z, x, core).
Axes of the slice: x: 2, y: 2, z: 4, core: 2. Of those that a mesh axis runs over, the one named last changes fastest.
Arguments:
- queries: bfloat16 [512, 24576], P(None, 'head'), may hold values from -100 to 100
- attn_keys: bfloat16 [4096, 24576], P('ctx', 'head'), may hold values from -6 to 6
- index_queries: bfloat16 [512, 8192], P(None, 'head'), may hold values from -16 to 16
- index_keys: bfloat16 [4096, 128], P('ctx'), may hold values from -6 to 6
- head_weights: float32 [512, 64], P(None, 'head'), may hold values from 0.1 to 1
- query_pos: int32 [512], replicated, may hold values from 16 to 32767
- key_offset: int32 [4096], P('ctx'), may hold values from 0 to 7
Outputs:
- index_query_grad: float32 [512, 8192], P('ctx', 'head')
- index_key_grad: float32 [4096, 128], P('ctx')
All inputs are finite; a program needn't handle non-finite values.
Results may differ from a plain program's by a relative error of at most 0.0027.
Values sent between devices are 32-bit elements; how exact they have to be, the bound alone decides.
A program may use at most 128 MiB of HBM per device.

v0:
```python
import math

import jax
import jax.numpy as jnp
from jax import lax
from jax.sharding import PartitionSpec as P

HEADS = 128
HEAD_DIM = 192
IDIM = 128
STRIDE = 8


NEG_FILL = -1e30


def combined_all(part, axis, combine):
    gathered = jax.tree.map(lambda a: lax.all_gather(a, axis), part)

    def take(source):
        return jax.tree.map(lambda a: lax.dynamic_index_in_dim(a, source, 0, False), gathered)

    return lax.fori_loop(
        1, lax.axis_size(axis), lambda source, state: combine(state, take(source)), take(0)
    )


def combine_stats(earlier, later):
    top_value = jnp.maximum(earlier[0], later[0])
    total_mass = earlier[1] * jnp.exp(earlier[0] - top_value) + later[1] * jnp.exp(
        later[0] - top_value
    )
    return (top_value, total_mass)


def row_stats(values, visible):
    masked = jnp.where(visible, values, NEG_FILL)
    local_top = jnp.max(masked, axis=-1)
    local_mass = jnp.sum(jnp.where(visible, jnp.exp(masked - local_top[..., None]), 0.0), axis=-1)
    top_value, total_mass = combined_all((local_top, local_mass), "ctx", combine_stats)
    return jnp.where(visible, jnp.exp(masked - top_value[..., None]), 0.0) / total_mass[..., None]


def shards(queries, attn_keys, index_queries, index_keys, head_weights, query_pos, key_offset):
    query_rows = queries.shape[0]
    key_rows = attn_keys.shape[0]
    local_heads = attn_keys.shape[1] // HEAD_DIM
    index_heads = index_queries.shape[1] // IDIM
    key_start = lax.axis_index("ctx") * key_rows
    key_pos = STRIDE * (key_start + jnp.arange(key_rows, dtype=jnp.int32)) + key_offset
    visible = key_pos[None, :] <= query_pos[:, None]
    attn_scale = 1.0 / math.sqrt(HEAD_DIM)
    inv_scale = 1.0 / math.sqrt(IDIM)
    query_heads = queries.reshape(query_rows, local_heads, HEAD_DIM)
    key_heads = attn_keys.reshape(key_rows, local_heads, HEAD_DIM)
    scores = (
        jnp.einsum("thd,shd->hts", query_heads, key_heads, preferred_element_type=jnp.float32)
        * attn_scale
    )
    head_probs = row_stats(scores, visible[None])
    target_part = jnp.sum(head_probs, axis=0)
    index_heads_q = index_queries.reshape(query_rows, index_heads, IDIM)
    activation = (
        jnp.einsum("tjd,sd->tjs", index_heads_q, index_keys, preferred_element_type=jnp.float32)
        * inv_scale
    )
    logit_part = jnp.sum(head_weights[:, :, None] * jnp.maximum(activation, 0.0), axis=1)
    target = lax.psum(target_part, "head") / HEADS
    logits = lax.psum(logit_part, "head")
    prob_step = row_stats(logits, visible) - target
    grad_terms = jnp.where(
        activation > 0.0, prob_step[:, None, :] * head_weights[:, :, None] * inv_scale, 0.0
    ).astype(jnp.bfloat16)
    key_part = jnp.einsum(
        "tjs,tjd->sd", grad_terms, index_heads_q, preferred_element_type=jnp.float32
    )
    key_grad = lax.psum(key_part, "head")
    result = jnp.einsum("tjs,sd->tjd", grad_terms, index_keys, preferred_element_type=jnp.float32)
    query_grad = lax.psum_scatter(
        result.reshape(
            query_rows // lax.axis_size("ctx") * lax.axis_size("ctx"), index_heads * IDIM
        ),
        "ctx",
        scatter_dimension=0,
        tiled=True,
    )
    return (query_grad, key_grad)


def solution(mesh):
    in_specs = (
        P(None, "head"),
        P("ctx", "head"),
        P(None, "head"),
        P("ctx", None),
        P(None, "head"),
        P(),
        P("ctx"),
    )
    out_specs = (P("ctx", "head"), P("ctx", None))
    return jax.shard_map(shards, mesh=mesh, in_specs=in_specs, out_specs=out_specs, check_vma=False)
```

profile of v0, /device:TPU:0, one launch (start us, length us, event | category | flops | bytes accessed | tf_op | source)
XLA Modules:
  0.0 419.4 jit_solution(3195242327979125005)
XLA Ops:
  7.2 0.7 multiply_add_fusion.1
  7.9 0.8 broadcast_compare_fusion
  8.7 0.2 copy.34
  9.0 16.7 %copy.35 = bf16[512,12288]{0,1:T(8,128)(2,1)} copy(bf16[512,12288]{1,0:T(8,128)(2,1)} %param.11) | data formatting | bytes 25165824 | tf_op args[0]
  25.7 8.7 %copy.36 = bf16[256,12288]{0,1:T(8,128)(2,1)} copy(bf16[256,12288]{1,0:T(8,128)(2,1)} %param.12) | data formatting | bytes 12582912 | tf_op args[1]
  34.3 20.6 %fusion.3 = (f32[64,512]{1,0:T(8,128)S(1)}, f32[64,512,256]{1,2,0:T(8,128)}) fusion(pred[512,256]{0,1:T(8,128)(4,1)S(1)} %copy.34, bf16[512,64,192]{0,2,1:T(8,128)(2,1)} %bitcast.63, bf16[256,64,192]{0,2,1:T(8,128)(2,1)} %bitcast.65), kind=kOutput, calls=%fused_computation.12 | convolution fusion | flops 3246358528 | bytes 52690944 | tf_op jit(solution)/shard_map/thd,shd->hts/dot_general | solution.py:57
  55.0 15.6 %select_reduce_fusion = f32[64,512]{1,0:T(8,128)} fusion(f32[64,512,256]{1,2,0:T(8,128)} %get-tuple-element.303, f32[64,512]{1,0:T(8,128)S(1)} %get-tuple-element.302, pred[512,256]{0,1:T(8,128)(4,1)S(1)} %copy.34), kind=kLoop, calls=%fused_computation.9 | loop fusion | flops 41910272 | bytes 33947648 | tf_op jit(solution)/shard_map/reduce_sum | solution.py:39
  70.6 0.0 all-gather.9.cloned.1.call-start
  70.6 0.7 all-gather.9.cloned.1.call-update
  71.4 5.4 %convert_reduce_fusion = (u32[512,256]{1,0:T(8,128)S(1)}, f32[512,32,256]{2,0,1:T(8,128)S(1)}) fusion(bf16[256,128]{1,0:T(8,128)(2,1)S(1)} %copy-done, bf16[512,4096]{1,0:T(8,128)(2,1)} %param.13), kind=kOutput, calls=%fused_computation.14 | convolution fusion | flops 1094582272 | bytes 21561344 | tf_op jit(solution)/shard_map/tjd,sd->tjs/dot_general | solution.py:64
  76.8 3.7 multiply_reduce_fusion
  80.4 34.5 %all-gather.11.cloned.1.call-done = f32[1024,512]{1,0:T(8,128)} async-done(((f32[64,512]{1,0:T(8,128)}), f32[1024,512]{1,0:T(8,128)}) %all-gather.11.cloned.1.call-update) | async-done | bytes 2097168 | tf_op jit(solution)/shard_map/all_gather | solution.py:18
  114.9 0.9 slice.13
  115.8 42.0 %all-gather.9.cloned.1.call-done = f32[1024,512]{1,0:T(8,128)} async-done(((f32[64,512]{1,0:T(8,128)}), f32[1024,512]{1,0:T(8,128)}) %all-gather.9.cloned.1.call-update) | async-done | bytes 2097168 | tf_op jit(solution)/shard_map/all_gather | solution.py:18
  157.8 0.9 slice.12
  158.8 16.6 %while.35 = (s32[]{:T(128)}, f32[64,512]{1,0:T(8,128)S(1)}, f32[64,512]{1,0:T(8,128)S(1)}, f32[16,64,512]{2,1,0:T(8,128)}, f32[16,64,512]{2,1,0:T(8,128)}, /*index=5*/s32[]{:T(128)}, s32[]{:T(128)}, s32[]{:T(128)}) while((s32[]{:T(128)}, f32[64,512]{1,0:T(8,128)S(1)}, f32[64,512]{1,0:T(8,128)S(1)}, f32[16,64,512]{2,1,0:T(8,128)}, ...), condition=%wide.region_9.10_spmd, body=%wide.region_8.9_spmd.sunk | while | flops 196613 | bytes 786563 | solution.py:23
  158.8 1.1 fusion.28
  159.9 1.1 fusion.28
  161.0 1.1 fusion.28
  162.1 1.1 fusion.28
  163.2 1.1 fusion.28
  164.3 1.1 fusion.28
  165.4 1.1 fusion.28
  166.5 1.1 fusion.28
  167.6 1.1 fusion.28
  168.8 1.1 fusion.28
  169.9 1.1 fusion.28
  171.0 1.1 fusion.28
  172.1 1.1 fusion.28
  173.2 1.1 fusion.28
  174.3 1.1 fusion.28
  175.4 15.3 %fusion.2 = f32[512,256]{0,1:T(8,128)S(1)} fusion(f32[64,512,256]{1,2,0:T(8,128)} %get-tuple-element.303, f32[64,512]{1,0:T(8,128)S(1)} %get-tuple-element.271, f32[64,512]{1,0:T(8,128)S(1)} %get-tuple-element.270, pred[512,256]{0,1:T(8,128)(4,1)S(1)} %copy.34), kind=kLoop, calls=%fused_computation.11 | loop fusion | flops 50200576 | bytes 34471936 | tf_op jit(solution)/shard_map/reduce_sum | solution.py:61
  190.7 1.0 copy.37
  191.8 0.0 all-reduce.4.cloned.1.call-start
  191.8 38.9 %all-reduce.6.cloned.1.call-done = (f32[512,256]{1,0:T(8,128)}, f32[512,256]{1,0:T(8,128)}) async-done(((f32[512,256]{1,0:T(8,128)}, f32[512,256]{1,0:T(8,128)}), (f32[512,256]{1,0:T(8,128)}, f32[512,256]{1,0:T(8,128)})) %all-reduce.6.cloned.1.call-update) | async-done | bytes 1048592 | tf_op jit(solution)/shard_map/psum | solution.py:68
  230.7 1.3 fusion.14
  232.0 1.3 select_reduce_fusion.1
  233.4 21.4 %all-gather.5 = f32[16,1,512]{2,1,0:T(1,128)S(1)} all-gather(f32[1,1,512]{2,1,0:T(1,128)S(1)} %bitcast.75), channel_id=3, replica_groups=mesh['head'=2,'ctx'=16] {'ctx'}, dimensions={0}, use_global_device_ids=true | all-gather | bytes 34816 | tf_op jit(solution)/shard_map/all_gather | solution.py:18
  254.8 17.7 %all-gather.4 = f32[16,1,512]{2,1,0:T(1,128)S(1)} all-gather(f32[1,1,512]{2,1,0:T(1,128)S(1)} %bitcast.74), channel_id=2, replica_groups=mesh['head'=2,'ctx'=16] {'ctx'}, dimensions={0}, use_global_device_ids=true | all-gather | bytes 34816 | tf_op jit(solution)/shard_map/all_gather | solution.py:18
  272.4 0.9 while.34
  273.3 1.5 multiply_subtract_fusion
  274.8 9.3 %fusion.11 = f32[256,128]{1,0:T(8,128)} fusion(u32[512,256]{1,0:T(8,128)S(1)} %get-tuple-element.300, f32[512,256]{1,0:T(8,128)S(1)} %multiply_subtract_fusion, f32[512,32]{0,1:T(8,128)S(1)} %copy-done.2, bf16[512,4096]{1,0:T(8,128)(2,1)} %param.13), kind=kOutput, calls=%fused_computation.24 | convolution fusion | flops 1103101952 | bytes 5439488 | tf_op jit(solution)/shard_map/tjs,tjd->sd/dot_general | solution.py:74
  284.2 0.0 reduce-scatter.2.cloned.1.call-start
  284.2 7.5 %fusion.5 = f32[512,32,128]{0,2,1:T(8,128)} fusion(u32[512,256]{1,0:T(8,128)S(1)} %get-tuple-element.300, f32[512,256]{1,0:T(8,128)S(1)} %multiply_subtract_fusion, f32[512,32]{0,1:T(8,128)S(1)} %copy-done.2, bf16[256,128]{1,0:T(8,128)(2,1)S(1)} %copy-done), kind=kOutput, calls=%fused_computation.18 | convolution fusion | flops 1103101952 | bytes 9568256 | tf_op jit(solution)/shard_map/tjs,sd->tjd/dot_general | solution.py:78
  291.7 9.0 %copy.39 = f32[512,4096]{1,0:T(8,128)} copy(f32[512,4096]{0,1:T(8,128)} %bitcast.64) | data formatting | bytes 16777216 | tf_op jit(solution)/shard_map/reshape | solution.py:80
  300.7 2.6 all-reduce.4.cloned.1.call-done
  303.3 108.0 %reduce-scatter.2.cloned.1.call-done = f32[32,4096]{1,0:T(8,128)} async-done(((f32[512,4096]{1,0:T(8,128)}), f32[32,4096]{1,0:T(8,128)}) %reduce-scatter.2.cloned.1.call-update) | async-done | bytes 524304 | tf_op jit(solution)/shard_map/reduce_scatter | solution.py:79
  411.3 1.6 copy.85
  (48 shorter events, 0.7 us)
Async XLA Ops:
  7.2 64.2 %copy-start = (bf16[256,128]{1,0:T(8,128)(2,1)S(1)}, bf16[256,128]{1,0:T(8,128)(2,1)}, u32[]{:S(2)}) copy-start(bf16[256,128]{1,0:T(8,128)(2,1)} %param.14) | copy-start | bytes 196612
  7.2 107.7 %all-gather.11.cloned.1.call-start = ((), (), s32[]{:S(2)}) async-start(), calls=%async_computation.4 | async-start | bytes 2228224 | tf_op jit(solution)/shard_map/all_gather | solution.py:18
  55.0 15.6 %copy-start.1 = (f32[64,512]{1,0:T(8,128)}, f32[64,512]{1,0:T(8,128)S(1)}, u32[]{:S(2)}) copy-start(f32[64,512]{1,0:T(8,128)S(1)} %get-tuple-element.302) | copy-start | bytes 393220
  70.5 6.2 %copy-start.2 = (f32[512,32]{0,1:T(8,128)S(1)}, f32[512,32]{0,1:T(8,128)}, u32[]{:S(2)}) copy-start(f32[512,32]{0,1:T(8,128)} %param.15) | copy-start | bytes 196612
  70.6 87.3 %all-gather.9.cloned.1.call-start = ((), (), s32[]{:S(2)}) async-start(), calls=%async_computation.3 | async-start | bytes 2228224 | tf_op jit(solution)/shard_map/all_gather | solution.py:18
  71.3 159.4 %all-reduce.6.cloned.1.call-start = ((), (), s32[]{:S(2)}) async-start(), calls=%async_computation.5 | async-start | bytes 2097152 | tf_op jit(solution)/shard_map/psum | solution.py:68
  175.4 55.3 %copy-start.3 = (s32[512]{0:T(512)S(1)}, s32[512]{0:T(512)}, u32[]{:S(2)}) copy-start(s32[512]{0:T(512)} %param.16) | copy-start | bytes 6148
  191.8 111.6 %all-reduce.4.cloned.1.call-start = ((), (), s32[]{:S(2)}) async-start(), calls=%async_computation.2 | async-start | bytes 262144 | tf_op jit(solution)/shard_map/psum | solution.py:77
  284.2 127.1 %reduce-scatter.2.cloned.1.call-start = ((), (), s32[]{:S(2)}) async-start(), calls=%async_computation.1 | async-start | bytes 8912896 | tf_op jit(solution)/shard_map/reduce_scatter | solution.py:79
Sparse Core Ops, SparseCore 0:
  70.7 44.1 all-gather.10
  117.6 40.1 all-gather.8
  191.9 38.8 all-reduce.5
  284.3 18.9 all-reduce.3
  307.8 103.4 reduce-scatter.1
where the time goes:
time: 421 us; the launch traced here: 419 us
  waiting for transfers between devices  227 us (54%)
  other arithmetic  56.8 us (13%)
  matrix products  42.8 us (10%)
  local copies, waits for them, and re-layouts  39.1 us (9%)
  blocking collectives  39.1 us (9%)
  between operations  13.9 us (3%)
    reduce_scatter x1, waiting for transfers between devices, shards(): lax.psum_scatter(result.reshape(query_rows // lax.axis_size('ctx') * lax....  108 us
    all_gather x2, waiting for transfers between devices, combined_all(): gathered = jax.tree.map(lambda a: lax.all_gather(a, axis), part)  76.5 us
    all_gather x2, blocking collectives, combined_all(): gathered = jax.tree.map(lambda a: lax.all_gather(a, axis), part)  39.1 us
    psum x1, waiting for transfers between devices, shards(): target = lax.psum(target_part, 'head') / HEADS  38.9 us
    unnamed x13, local copies, waits for them, and re-layouts  27 us
    dot_general x1, matrix products, shards(): jnp.einsum('thd,shd->hts', query_heads, key_heads, preferred_element_type...  20.6 us
    reduce_sum x2, other arithmetic, row_stats(): jnp.sum(jnp.where(visible, jnp.exp(masked - local_top[..., None]), 0.0),...  16.9 us
    add x30, other arithmetic, combine_stats(): earlier[1] * jnp.exp(earlier[0] - top_value)  16.6 us
  transfers between devices with their start and end apart: 5, of which 5 were waited for; matrix products, arithmetic and copies ran while one was open for 6% of the time, Pallas kernels for 0%

commit v1 on v0

v1 whole, which is shorter than its diff:
```python
import functools
import math

import jax
import jax.numpy as jnp
from jax import lax
from jax.experimental import pallas as pl
from jax.experimental.pallas import tpu as pltpu
from jax.sharding import PartitionSpec as P

HEADS = 128
HEAD_DIM = 192
IDIM = 128
STRIDE = 8
NEG_FILL = -1e30
LOG2E = math.log2(math.e)
BLOCKS = 4
MESH = pl.DeviceIdType.MESH
F32 = jnp.float32
BF16 = jnp.bfloat16
NT = (((1,), (1,)), ((), ()))


def matmul_nt(a, b):
    return lax.dot_general(a, b, NT, preferred_element_type=F32)


def kernel(
    n_ctx, n_head, heads,
    q_hbm, k_hbm, iq_hbm, ik_ref, hwt_ref, hwcol_ref, qpos_ref, koff_ref,
    qgrad_ref, kgrad_ref,
    q_v, k_v, iq_v, probs, ikg, bias, lg_part, lg_recv, expo,
    stat_send, stat_recv, ist_send, ist_recv, w_send, w_recv, wi_ref,
    tg_part, tg_recv, pst, ps_send, ps_recv, kg_part, kg_recv, qg, hwb, iqo,
    q_sem, k_sem, iq_sem, ag_s, ag_r, lg_s, lg_r, st_s, st_r, is_s, is_r,
    w_s, w_r, tg_s, tg_r, ps_s, ps_r, kg_s, kg_r,
):
    me = lax.axis_index("ctx")
    my_head = lax.axis_index("head")
    pairs, rows, pair_width = q_v.shape
    keys = k_v.shape[1]
    iheads = iq_v.shape[0]
    own = rows // n_ctx
    per_owner = max(1, 2 * pairs // n_ctx)
    split = n_ctx * per_owner // (2 * pairs)
    part_rows = rows // split
    half = keys // 2
    block = keys // BLOCKS
    score_scale = LOG2E / math.sqrt(HEAD_DIM)
    inv_scale = 1.0 / math.sqrt(IDIM)

    def peer_of(k, n, base):
        return lax.rem(base + k, n)

    def q_copy(p):
        cols = pl.ds(pl.multiple_of(p * pair_width, 128), pair_width)
        return pltpu.make_async_copy(q_hbm.at[:, cols], q_v.at[p], q_sem.at[p])

    def k_copy(p):
        cols = pl.ds(pl.multiple_of(p * pair_width, 128), pair_width)
        return pltpu.make_async_copy(k_hbm.at[:, cols], k_v.at[p], k_sem.at[p])

    def iq_copy(j):
        cols = pl.ds(pl.multiple_of(j * IDIM, 128), IDIM)
        return pltpu.make_async_copy(iq_hbm.at[:, cols], iq_v.at[j], iq_sem.at[j])

    @pl.loop(0, iheads)
    def _(j):
        iq_copy(j).start()

    @pl.loop(0, pairs)
    def _(p):
        q_copy(p).start()
        k_copy(p).start()

    barrier = pltpu.get_barrier_semaphore()
    for k in range(1, n_ctx):
        pl.semaphore_signal(
            barrier, inc=1, device_id={"ctx": peer_of(k, n_ctx, me)}, device_id_type=MESH
        )
    for k in range(1, n_head):
        pl.semaphore_signal(
            barrier, inc=1, device_id={"head": peer_of(k, n_head, my_head)}, device_id_type=MESH
        )

    ikg[me] = ik_ref[...].astype(F32)
    key_pos = STRIDE * (me * keys + lax.broadcasted_iota(jnp.int32, (keys, 1), 0)) + koff_ref[...]
    bias[...] = jnp.where(key_pos <= qpos_ref[...], 0.0, NEG_FILL)
    hwb[...] = jnp.broadcast_to(hwcol_ref[...] * inv_scale, hwb.shape)
    lg_part[...] = jnp.zeros_like(lg_part)

    pl.semaphore_wait(barrier, n_ctx - 1 + n_head - 1)

    bits = [1 << b for b in reversed(range(n_ctx.bit_length() - 1))]

    def flip(index, bit):
        return index + bit * (1 - 2 * lax.rem(lax.div(index, bit), 2))

    def ag_shards(stage, base):
        shards = [base]
        for bit in bits[:stage]:
            shards = shards + [flip(s, bit) for s in shards]
        return shards

    def ag_copy(shard, stage):
        return pltpu.make_async_remote_copy(
            src_ref=ikg.at[shard], dst_ref=ikg.at[shard],
            send_sem=ag_s.at[stage, shard], recv_sem=ag_r.at[shard],
            device_id={"ctx": flip(me, bits[stage])}, device_id_type=MESH,
        )

    def ag_start(stage):
        for shard in ag_shards(stage, me):
            ag_copy(shard, stage).start()

    def ag_recv(stage):
        for shard in ag_shards(stage, flip(me, bits[stage])):
            ag_copy(shard, stage).wait_recv()

    def ag_sent(stage):
        for shard in ag_shards(stage, me):
            ag_copy(shard, stage).wait_send()

    stages = len(bits)
    ag_start(0)

    @pl.loop(0, iheads)
    def _(j):
        iq_copy(j).wait()
        act = matmul_nt(ik_ref[...], iq_v[j])
        weight = hwt_ref[pl.ds(j, 1), :] * inv_scale
        lg_part[...] += weight * jnp.maximum(act, 0.0)

    def head_copy(k, src, dst, send, recv):
        return pltpu.make_async_remote_copy(
            src_ref=src, dst_ref=dst, send_sem=send, recv_sem=recv,
            device_id={"head": peer_of(k, n_head, my_head)}, device_id_type=MESH,
        )

    def lg_copy(k, slot):
        return head_copy(k, lg_part, lg_recv.at[slot], lg_s.at[k], lg_r.at[slot])

    for k in range(1, n_head):
        lg_copy(k, my_head).start()

    column = lax.broadcasted_iota(jnp.int32, (keys, 256), 1)

    def attn_pair(p):
        q_copy(p).wait()
        k_copy(p).wait()
        for a in range(2):
            kept = column < HEAD_DIM if a == 0 else column >= 256 - HEAD_DIM
            k_head = k_v[p, :, a * 128 : a * 128 + 256]
            k_head = jnp.where(kept, k_head, jnp.zeros_like(k_head))
            scores = matmul_nt(k_head, q_v[p, :, a * 128 : a * 128 + 256])
            scores = scores * score_scale + bias[...]
            top = jnp.max(scores, axis=0, keepdims=True)
            expo_head = jnp.exp2(scores - top)
            mass = jnp.sum(expo_head, axis=0, keepdims=True)
            head = 2 * p + a
            probs[head] = expo_head.astype(BF16)
            owner = lax.div(head, per_owner) * split
            row = lax.rem(head, per_owner)
            for part in range(split):
                lanes = slice(part * part_rows, (part + 1) * part_rows)
                stat_send[owner + part, pl.ds(row, 1), :] = top[:, lanes]
                stat_send[owner + part, pl.ds(row + per_owner, 1), :] = mass[:, lanes]

    cuts = [pairs * s // (stages - 1) for s in range(stages)]
    for s in range(stages - 1):
        pl.loop(cuts[s], cuts[s + 1])(attn_pair)
        ag_recv(s)
        ag_start(s + 1)

    for k in range(1, n_head):
        slot = peer_of(k, n_head, my_head)
        lg_copy(k, slot).wait_recv()
    logits = lg_part[...]
    for k in range(1, n_head):
        logits = logits + lg_recv[peer_of(k, n_head, my_head)]
    logits = logits * LOG2E + bias[...]
    itop = jnp.max(logits, axis=0, keepdims=True)
    logits = jnp.exp2(logits - itop)
    expo[...] = logits
    ist_send[0:1, :] = itop
    ist_send[1:2, :] = jnp.sum(logits, axis=0, keepdims=True)

    def ctx_copy(k, src, dst, send, recv):
        return pltpu.make_async_remote_copy(
            src_ref=src, dst_ref=dst, send_sem=send, recv_sem=recv,
            device_id={"ctx": peer_of(k, n_ctx, me)}, device_id_type=MESH,
        )

    def stat_copy(k, peer, slot):
        return ctx_copy(k, stat_send.at[peer], stat_recv.at[slot], st_s.at[k], st_r.at[slot])

    def ist_copy(k, slot):
        return ctx_copy(k, ist_send, ist_recv.at[slot], is_s.at[k], is_r.at[slot])

    def w_copy(k, peer, slot):
        return ctx_copy(k, w_send.at[peer], w_recv.at[slot], w_s.at[k], w_r.at[slot])

    def ps_copy(c, k, peer, slot):
        return ctx_copy(
            k, ps_send.at[c, peer], ps_recv.at[c, slot], ps_s.at[c, k], ps_r.at[c, slot]
        )

    @pl.loop(1, n_ctx)
    def _(k):
        peer = peer_of(k, n_ctx, me)
        stat_copy(k, peer, me).start()
        ist_copy(k, me).start()

    stat_recv[me] = stat_send[me]
    ist_recv[me] = ist_send[...]

    @pl.loop(1, n_ctx)
    def _(k):
        peer = peer_of(k, n_ctx, me)
        stat_copy(k, peer, peer).wait_recv()

    tops = stat_recv[:, :per_owner, :]
    masses = stat_recv[:, per_owner:, :]
    top = jnp.max(tops, axis=0, keepdims=True)
    shift = jnp.exp2(tops - top)
    total = jnp.sum(masses * shift, axis=0, keepdims=True)
    w_send[...] = shift * (1.0 / (HEADS * total))

    @pl.loop(1, n_ctx)
    def _(k):
        peer = peer_of(k, n_ctx, me)
        w_copy(k, peer, me).start()

    w_recv[me] = w_send[me]

    @pl.loop(1, n_ctx)
    def _(k):
        peer = peer_of(k, n_ctx, me)
        ist_copy(k, peer).wait_recv()

    itops = ist_recv[:, 0:1, :]
    imasses = ist_recv[:, 1:2, :]
    itop_all = jnp.max(itops, axis=0)
    itotal = jnp.sum(imasses * jnp.exp2(itops - itop_all[None]), axis=0)
    wi_ref[...] = jnp.exp2(ist_send[0:1, :] - itop_all) / itotal

    @pl.loop(1, n_ctx)
    def _(k):
        peer = peer_of(k, n_ctx, me)
        w_copy(k, peer, peer).wait_recv()

    def tg_copy(k, b, slot):
        span = pl.ds(b * block, block)
        return head_copy(
            k, tg_part.at[span], tg_recv.at[slot, span], tg_s.at[b, k], tg_r.at[b, slot]
        )

    for b in range(BLOCKS):
        for c in range(rows // 256):
            lanes = slice(c * 256, (c + 1) * 256)

            part, start = c * 256 // part_rows, c * 256 % part_rows

            def add_owner(o, acc):
                weights = w_recv[o * split + part, :, start : start + 256]
                for r in range(per_owner):
                    terms = probs[o * per_owner + r, b * block : (b + 1) * block, lanes]
                    acc = acc + terms.astype(F32) * weights[r : r + 1]
                return acc

            tg_part[b * block : (b + 1) * block, lanes] = lax.fori_loop(
                0, n_ctx // split, add_owner, jnp.zeros((block, 256), F32)
            )
        for k in range(1, n_head):
            tg_copy(k, b, my_head).start()

    for s in range(stages - 1, stages):
        ag_recv(s)

    for c in range(2):
        for b in range(c * BLOCKS // 2, (c + 1) * BLOCKS // 2):
            for k in range(1, n_head):
                tg_copy(k, b, peer_of(k, n_head, my_head)).wait_recv()
        span = slice(c * half, (c + 1) * half)
        target = tg_part[span]
        for k in range(1, n_head):
            target = target + tg_recv[peer_of(k, n_head, my_head), span]
        step = expo[span] * wi_ref[...] - target
        pst[span] = step
        ps_send[c] = step.T.reshape(n_ctx, own, half)

        @pl.loop(1, n_ctx)
        def _(k):
            peer = peer_of(k, n_ctx, me)
            ps_copy(c, k, peer, me).start()

        ps_recv[c, me] = ps_send[c, me]

    kg_part[...] = jnp.zeros_like(kg_part)

    @pl.loop(0, iheads)
    def _(j):
        act = matmul_nt(ik_ref[...], iq_v[j])
        weight = hwt_ref[pl.ds(j, 1), :] * inv_scale
        terms = jnp.where(act > 0.0, pst[...] * weight, 0.0).astype(BF16)
        kg_part[...] += jnp.dot(terms, iq_v[j], preferred_element_type=F32)

    def kg_copy(k, slot):
        return head_copy(k, kg_part, kg_recv.at[slot], kg_s.at[k], kg_r.at[slot])

    for k in range(1, n_head):
        kg_copy(k, my_head).start()

    first = pl.multiple_of(me * own, own)
    for j in range(iheads):
        iqo[j * own : (j + 1) * own, :] = iq_v[j, pl.ds(first, own), :]
    qg[...] = jnp.zeros_like(qg)

    def add_source(source):
        source_keys = ikg[source].astype(BF16)
        act = matmul_nt(iqo[...], source_keys)
        terms = []
        for c in range(2):
            step = ps_recv[c, source]
            weighted = hwb[...].reshape(iheads, own, half) * step[None]
            positive = act[:, c * half : (c + 1) * half] > 0.0
            terms.append(
                jnp.where(positive, weighted.reshape(iheads * own, half), 0.0).astype(BF16)
            )
        qg[...] += jnp.dot(
            jnp.concatenate(terms, axis=1), source_keys, preferred_element_type=F32
        )

    add_source(me)

    @pl.loop(1, n_ctx)
    def _(k):
        source = peer_of(k, n_ctx, me)
        for c in range(2):
            ps_copy(c, k, source, source).wait_recv()
        add_source(source)

    for j in range(iheads):
        qgrad_ref[:, j * IDIM : (j + 1) * IDIM] = qg[j * own : (j + 1) * own, :]

    key_grad = kg_part[...]
    for k in range(1, n_head):
        slot = peer_of(k, n_head, my_head)
        kg_copy(k, slot).wait_recv()
        key_grad = key_grad + kg_recv[slot]
    kgrad_ref[...] = key_grad

    for s in range(stages):
        ag_sent(s)
    for k in range(1, n_head):
        lg_copy(k, my_head).wait_send()
        kg_copy(k, my_head).wait_send()
        for b in range(BLOCKS):
            tg_copy(k, b, my_head).wait_send()

    @pl.loop(1, n_ctx)
    def _(k):
        peer = peer_of(k, n_ctx, me)
        stat_copy(k, peer, me).wait_send()
        ist_copy(k, me).wait_send()
        w_copy(k, peer, me).wait_send()
        for c in range(2):
            ps_copy(c, k, peer, me).wait_send()


def shards(n_ctx, n_head, queries, attn_keys, index_queries, index_keys, head_weights, query_pos, key_offset):
    rows = queries.shape[0]
    keys = attn_keys.shape[0]
    heads = attn_keys.shape[1] // HEAD_DIM
    iheads = index_queries.shape[1] // IDIM
    own = rows // n_ctx
    pairs = heads // 2
    per_owner = max(1, heads // n_ctx)
    split = n_ctx * per_owner // heads
    stages = n_ctx.bit_length() - 1
    own_weights = lax.dynamic_slice_in_dim(head_weights, lax.axis_index("ctx") * own, own, 0)
    weight_col = own_weights.T.reshape(iheads * own, 1)
    vmem = pltpu.VMEM
    dma = pltpu.SemaphoreType.DMA
    any_space = pl.BlockSpec(memory_space=pl.ANY)
    vmem_space = pl.BlockSpec(memory_space=pltpu.VMEM)
    return pl.pallas_call(
        functools.partial(kernel, n_ctx, n_head, heads),
        out_shape=(
            jax.ShapeDtypeStruct((own, iheads * IDIM), F32),
            jax.ShapeDtypeStruct((keys, IDIM), F32),
        ),
        in_specs=[any_space] * 3 + [vmem_space] * 5,
        out_specs=(vmem_space, vmem_space),
        scratch_shapes=[
            vmem((pairs, rows, 2 * HEAD_DIM), BF16),
            vmem((pairs, keys, 2 * HEAD_DIM), BF16),
            vmem((iheads, rows, IDIM), BF16),
            vmem((heads, keys, rows), BF16),
            vmem((n_ctx, keys, IDIM), F32),
            vmem((keys, rows), F32),
            vmem((keys, rows), F32),
            vmem((n_head, keys, rows), F32),
            vmem((keys, rows), F32),
            vmem((n_ctx, 2 * per_owner, rows // split), F32),
            vmem((n_ctx, 2 * per_owner, rows // split), F32),
            vmem((2, rows), F32),
            vmem((n_ctx, 2, rows), F32),
            vmem((n_ctx, per_owner, rows // split), F32),
            vmem((n_ctx, per_owner, rows // split), F32),
            vmem((1, rows), F32),
            vmem((keys, rows), F32),
            vmem((n_head, keys, rows), F32),
            vmem((keys, rows), F32),
            vmem((2, n_ctx, own, keys // 2), F32),
            vmem((2, n_ctx, own, keys // 2), F32),
            vmem((keys, IDIM), F32),
            vmem((n_head, keys, IDIM), F32),
            vmem((iheads * own, IDIM), F32),
            vmem((iheads * own, keys // 2), F32),
            vmem((iheads * own, IDIM), BF16),
            dma((pairs,)),
            dma((pairs,)),
            dma((iheads,)),
            dma((stages, n_ctx)),
            dma((n_ctx,)),
            dma((n_head,)),
            dma((n_head,)),
            dma((n_ctx,)),
            dma((n_ctx,)),
            dma((n_ctx,)),
            dma((n_ctx,)),
            dma((n_ctx,)),
            dma((n_ctx,)),
            dma((BLOCKS, n_head)),
            dma((BLOCKS, n_head)),
            dma((2, n_ctx)),
            dma((2, n_ctx)),
            dma((n_head,)),
            dma((n_head,)),
        ],
        compiler_params=pltpu.CompilerParams(
            collective_id=0, has_side_effects=True, vmem_limit_bytes=64 * 1024 * 1024 - 65536
        ),
    )(
        queries,
        attn_keys,
        index_queries,
        index_keys,
        head_weights.T,
        weight_col,
        query_pos.reshape(1, rows),
        key_offset.reshape(keys, 1),
    )


def solution(mesh):
    in_specs = (
        P(None, "head"),
        P("ctx", "head"),
        P(None, "head"),
        P("ctx", None),
        P(None, "head"),
        P(),
        P("ctx"),
    )
    out_specs = (P("ctx", "head"), P("ctx", None))
    body = functools.partial(shards, mesh.shape["ctx"], mesh.shape["head"])
    return jax.shard_map(body, mesh=mesh, in_specs=in_specs, out_specs=out_specs, check_vma=False)
```

time: 421 us -> 101 us (0.24)
  waiting for transfers between devices: 227 us -> 0 us
  Pallas kernels: 0 us -> 93.1 us
  other arithmetic: 56.8 us -> 0 us
  matrix products: 42.8 us -> 0 us
  blocking collectives: 39.1 us -> 0 us
  local copies, waits for them, and re-layouts: 39.1 us -> 7.04 us
  between operations: 13.9 us -> 0.64 us
    reduce_scatter x1 -> x0, waiting for transfers between devices: 108 us -> none  [shards(): lax.psum_scatter(result.reshape(query_rows // lax.axis_size('ctx') * lax....]
    pallas_call x0 -> x1, Pallas kernels: none -> 93.1 us  [shards(): pl.pallas_call(functools.partial(kernel, n_ctx, n_head, heads), out_shape...]
    all_gather x2 -> x0, waiting for transfers between devices: 76.5 us -> none  [combined_all(): gathered = jax.tree.map(lambda a: lax.all_gather(a, axis), part)]
    dot_general x4 -> x0, matrix products: 42.8 us -> none  [the longest x1 20.6 us: shards(): jnp.einsum('thd,shd->hts', query_heads, key_heads, preferred_element_type...]
    psum x2 -> x0, waiting for transfers between devices: 41.6 us -> none  [the longest x1 38.9 us: shards(): target = lax.psum(target_part, 'head') / HEADS]
    all_gather x2 -> x0, blocking collectives: 39.1 us -> none  [combined_all(): gathered = jax.tree.map(lambda a: lax.all_gather(a, axis), part)]
    reduce_sum x4 -> x0, other arithmetic: 35.9 us -> none  [the longest x2 16.9 us: row_stats(): jnp.sum(jnp.where(visible, jnp.exp(masked - local_top[..., None]), 0.0),...]
    unnamed x13 -> x2, local copies, waits for them, and re-layouts: 27 us -> 3.44 us
  transfers between devices with their start and end apart: 5 -> 0, of which waited for: 5 -> 0; matrix products, arithmetic and copies ran while one was open for 6% -> 0% of each run, Pallas kernels for 0% -> 0%
where the time goes in v1:
time: 101 us
  Pallas kernels  93.1 us (92%)
  local copies, waits for them, and re-layouts  7.04 us (7%)
    pallas_call x1, Pallas kernels, shards(): pl.pallas_call(functools.partial(kernel, n_ctx, n_head, heads), out_shape...  93.1 us
    unnamed x2, local copies, waits for them, and re-layouts  3.44 us

profile of v1, /device:TPU:0, one launch (start us, length us, event | category | flops | bytes accessed | tf_op | source)
XLA Modules:
  0.0 100.8 jit_solution(2168001873183710428)
XLA Ops:
  0.6 0.8 dynamic-slice_bitcast_fusion
  1.4 1.5 %copy.10.koff_ref = s32[256,1]{1,0:T(8,128)} copy(s32[256,1]{0,1:T(1,128)} %bitcast.7) | data formatting | bytes 2048 | tf_op jit(solution)/shard_map/reshape | solution.py:453
  2.9 1.3 %reshape.16.hwcol_ref = f32[1024,1]{1,0:T(8,128)} reshape(f32[32,32]{1,0:T(8,128)S(1)} %dynamic-slice_bitcast_fusion) | data formatting | bytes 8192 | tf_op jit(solution)/shard_map/reshape | solution.py:382
  4.2 93.1 %shard_map.86 = (f32[32,4096]{1,0:T(8,128)}, f32[256,128]{1,0:T(8,128)}) custom-call(bf16[512,12288]{1,0:T(8,128)(2,1)} %q_hbm.1, bf16[256,12288]{1,0:T(8,128)(2,1)} %k_hbm.1, bf16[512,4096]{1,0:T(8,128)(2,1)} %iq_hbm.1, bf16[256,128]{1,0:T(8,128)(2,1)} %ik_ref.1, f32[32,512]{1,0:T(8,128)} %bitcast.5, f32[1024,1]{1,0:T(8,128)} %reshape.16.hwcol_ref, ...), custom_call_target="tpu_custom_call" | custom-call | tf_op jit(solution)/shard_map/pallas_call | solution.py:387
  97.3 1.9 %copy.13 = f32[32,4096]{1,0:T(8,128)} copy(f32[32,4096]{1,0:T(8,128)} %get-tuple-element.4) | data formatting | bytes 1048576
  99.2 1.6 %copy.14 = f32[256,128]{1,0:T(8,128)} copy(f32[256,128]{1,0:T(8,128)} %get-tuple-element.5) | data formatting | bytes 262144

commit v2 on v1

v2 whole, which is shorter than its diff:
```python
import functools
import math

import jax
import jax.numpy as jnp
from jax import lax
from jax.experimental import pallas as pl
from jax.experimental.pallas import tpu as pltpu
from jax.sharding import PartitionSpec as P

HEADS = 128
HEAD_DIM = 192
IDIM = 128
STRIDE = 8
NEG_FILL = -1e30
LOG2E = math.log2(math.e)
BLOCKS = 2
MESH = pl.DeviceIdType.MESH
F32 = jnp.float32
BF16 = jnp.bfloat16
NT = (((1,), (1,)), ((), ()))


def matmul_nt(a, b):
    return lax.dot_general(a, b, NT, preferred_element_type=F32)


def kernel(
    n_ctx, n_head, heads,
    q_hbm, k_hbm, iq_hbm, ik_ref, hwt_ref, qpos_ref, koff_ref,
    qgrad_ref, kgrad_ref,
    q_v, k_v, iq_v, probs, ikg, bias, lg_part, lg_recv, expo,
    stat_send, stat_recv, ist_send, ist_recv, w_send, w_recv, wi_ref,
    tg_part, tg_recv, pst, ps_send, ps_recv, kg_part, kg_recv, qg, hwb, hw_rows, iqo,
    q_sem, k_sem, iq_sem, ag_s, ag_r, lg_s, lg_r, st_s, st_r, is_s, is_r,
    w_s, w_r, tg_s, tg_r, ps_s, ps_r, kg_s, kg_r,
):
    me = lax.axis_index("ctx")
    my_head = lax.axis_index("head")
    pairs, rows, pair_width = q_v.shape
    keys = k_v.shape[1]
    iheads = iq_v.shape[0]
    own = rows // n_ctx
    per_owner = max(1, 2 * pairs // n_ctx)
    split = n_ctx * per_owner // (2 * pairs)
    lanes_half = rows // 2
    part_rows = lanes_half // split
    block = keys // BLOCKS
    score_scale = LOG2E / math.sqrt(HEAD_DIM)
    inv_scale = 1.0 / math.sqrt(IDIM)

    def peer_of(k, n, base):
        return lax.rem(base + k, n)

    def q_copy(p):
        cols = pl.ds(pl.multiple_of(p * pair_width, 128), pair_width)
        return pltpu.make_async_copy(q_hbm.at[:, cols], q_v.at[p], q_sem.at[p])

    def k_copy(p):
        cols = pl.ds(pl.multiple_of(p * pair_width, 128), pair_width)
        return pltpu.make_async_copy(k_hbm.at[:, cols], k_v.at[p], k_sem.at[p])

    def iq_copy(j):
        cols = pl.ds(pl.multiple_of(j * IDIM, 128), IDIM)
        return pltpu.make_async_copy(iq_hbm.at[:, cols], iq_v.at[j], iq_sem.at[j])

    @pl.loop(0, iheads)
    def _(j):
        iq_copy(j).start()

    @pl.loop(0, pairs)
    def _(p):
        q_copy(p).start()
        k_copy(p).start()

    barrier = pltpu.get_barrier_semaphore()
    for k in range(1, n_ctx):
        pl.semaphore_signal(
            barrier, inc=1, device_id={"ctx": peer_of(k, n_ctx, me)}, device_id_type=MESH
        )
    for k in range(1, n_head):
        pl.semaphore_signal(
            barrier, inc=1, device_id={"head": peer_of(k, n_head, my_head)}, device_id_type=MESH
        )

    ikg[me] = ik_ref[...].astype(F32)
    offset = jnp.broadcast_to(koff_ref[...].astype(F32), (128, keys)).T[:, 0:1].astype(jnp.int32)
    key_pos = STRIDE * (me * keys + lax.broadcasted_iota(jnp.int32, (keys, 1), 0)) + offset
    bias[...] = jnp.where(key_pos <= qpos_ref[...], 0.0, NEG_FILL)
    hw_rows[...] = hwt_ref[...].T * inv_scale
    own_weights = hw_rows[pl.ds(pl.multiple_of(me * own, own), own), :]
    for j in range(iheads):
        hwb[j * own : (j + 1) * own, :] = jnp.broadcast_to(own_weights[:, j : j + 1], (own, 128))
    lg_part[...] = jnp.zeros_like(lg_part)

    pl.semaphore_wait(barrier, n_ctx - 1 + n_head - 1)

    bits = [1 << b for b in reversed(range(n_ctx.bit_length() - 1))]

    def flip(index, bit):
        return index + bit * (1 - 2 * lax.rem(lax.div(index, bit), 2))

    def ag_shards(stage, base):
        shards = [base]
        for bit in bits[:stage]:
            shards = shards + [flip(s, bit) for s in shards]
        return shards

    sub_rows = keys // 2

    def ag_copy(shard, sub, stage):
        piece = ikg.at[shard, pl.ds(sub * sub_rows, sub_rows)]
        return pltpu.make_async_remote_copy(
            src_ref=piece, dst_ref=piece,
            send_sem=ag_s.at[stage, sub, shard], recv_sem=ag_r.at[sub, shard],
            device_id={"ctx": flip(me, bits[stage])}, device_id_type=MESH,
        )

    def ag_start(sub, stage):
        for shard in ag_shards(stage, me):
            ag_copy(shard, sub, stage).start()

    def ag_recv(sub, stage):
        for shard in ag_shards(stage, flip(me, bits[stage])):
            ag_copy(shard, sub, stage).wait_recv()

    def ag_sent(sub, stage):
        for shard in ag_shards(stage, me):
            ag_copy(shard, sub, stage).wait_send()

    def ag_forward(event):
        sub, stage = event % 2, event // 2
        ag_recv(sub, stage)
        ag_start(sub, stage + 1)

    stages = len(bits)
    forwards = 2 * (stages - 1)
    for sub in range(2):
        ag_start(sub, 0)

    @pl.loop(0, iheads)
    def _(j):
        iq_copy(j).wait()
        act = matmul_nt(ik_ref[...], iq_v[j])
        weight = hwt_ref[pl.ds(j, 1), :] * inv_scale
        lg_part[...] += weight * jnp.maximum(act, 0.0)

    def head_copy(k, src, dst, send, recv):
        return pltpu.make_async_remote_copy(
            src_ref=src, dst_ref=dst, send_sem=send, recv_sem=recv,
            device_id={"head": peer_of(k, n_head, my_head)}, device_id_type=MESH,
        )

    def lg_copy(k, slot):
        return head_copy(k, lg_part, lg_recv.at[slot], lg_s.at[k], lg_r.at[slot])

    for k in range(1, n_head):
        lg_copy(k, my_head).start()

    def ctx_copy(k, src, dst, send, recv):
        return pltpu.make_async_remote_copy(
            src_ref=src, dst_ref=dst, send_sem=send, recv_sem=recv,
            device_id={"ctx": peer_of(k, n_ctx, me)}, device_id_type=MESH,
        )

    def stat_copy(h, k, peer, slot):
        return ctx_copy(
            k, stat_send.at[h, peer], stat_recv.at[h, slot], st_s.at[h, k], st_r.at[h, slot]
        )

    def ist_copy(k, slot):
        return ctx_copy(k, ist_send, ist_recv.at[slot], is_s.at[k], is_r.at[slot])

    def w_copy(h, k, peer, slot):
        return ctx_copy(k, w_send.at[h, peer], w_recv.at[h, slot], w_s.at[h, k], w_r.at[h, slot])

    def ps_copy(peer, slot):
        return pltpu.make_async_remote_copy(
            src_ref=ps_send.at[peer], dst_ref=ps_recv.at[slot],
            send_sem=ps_s.at[peer], recv_sem=ps_r.at[slot],
            device_id={"ctx": peer}, device_id_type=MESH,
        )

    def send_stats(h):
        @pl.loop(1, n_ctx)
        def _(k):
            stat_copy(h, k, peer_of(k, n_ctx, me), me).start()

        stat_recv[h, me] = stat_send[h, me]

    def send_weights(h):
        @pl.loop(1, n_ctx)
        def _(k):
            peer = peer_of(k, n_ctx, me)
            stat_copy(h, k, peer, peer).wait_recv()

        tops = stat_recv[h, :, :per_owner, :]
        masses = stat_recv[h, :, per_owner:, :]
        top = jnp.max(tops, axis=0, keepdims=True)
        shift = jnp.exp2(tops - top)
        total = jnp.sum(masses * shift, axis=0, keepdims=True)
        w_send[h] = shift * (1.0 / (HEADS * total))

        @pl.loop(1, n_ctx)
        def _(k):
            w_copy(h, k, peer_of(k, n_ctx, me), me).start()

        w_recv[h, me] = w_send[h, me]

    def recv_weights(h):
        @pl.loop(1, n_ctx)
        def _(k):
            peer = peer_of(k, n_ctx, me)
            w_copy(h, k, peer, peer).wait_recv()

    column = lax.broadcasted_iota(jnp.int32, (keys, 256), 1)

    def attn_pair(h, p):
        span = slice(h * lanes_half, (h + 1) * lanes_half)
        for a in range(2):
            kept = column < HEAD_DIM if a == 0 else column >= 256 - HEAD_DIM
            k_head = k_v[p, :, a * 128 : a * 128 + 256]
            k_head = jnp.where(kept, k_head, jnp.zeros_like(k_head))
            scores = matmul_nt(k_head, q_v[p, span, a * 128 : a * 128 + 256])
            scores = scores * score_scale + bias[:, span]
            top = jnp.max(scores, axis=0, keepdims=True)
            expo_head = jnp.exp2(scores - top)
            mass = jnp.sum(expo_head, axis=0, keepdims=True)
            head = 2 * p + a
            probs[head, :, span] = expo_head.astype(BF16)
            owner = lax.div(head, per_owner) * split
            row = lax.rem(head, per_owner)
            for part in range(split):
                lanes = slice(part * part_rows, (part + 1) * part_rows)
                stat_send[h, owner + part, pl.ds(row, 1), :] = top[:, lanes]
                stat_send[h, owner + part, pl.ds(row + per_owner, 1), :] = mass[:, lanes]

    ag_forward(0)
    for h in range(2):
        events = {}
        for event in range(1, forwards):
            at = event * 2 * pairs // forwards
            if at // pairs == h:
                events.setdefault(at % pairs, []).append(event)

        @pl.loop(0, pairs)
        def _(p):
            if h == 0:
                q_copy(p).wait()
                k_copy(p).wait()
            attn_pair(h, p)
            if h == 1:
                pl.when(p == pairs // 2)(functools.partial(send_weights, 0))
            for at, forwarded in events.items():

                @pl.when(p == at)
                def _():
                    for event in forwarded:
                        ag_forward(event)

        send_stats(h)

    for k in range(1, n_head):
        slot = peer_of(k, n_head, my_head)
        lg_copy(k, slot).wait_recv()
    logits = lg_part[...]
    for k in range(1, n_head):
        logits = logits + lg_recv[peer_of(k, n_head, my_head)]
    logits = logits * LOG2E + bias[...]
    itop = jnp.max(logits, axis=0, keepdims=True)
    logits = jnp.exp2(logits - itop)
    expo[...] = logits
    ist_send[0:1, :] = itop
    ist_send[1:2, :] = jnp.sum(logits, axis=0, keepdims=True)

    @pl.loop(1, n_ctx)
    def _(k):
        ist_copy(k, me).start()

    ist_recv[me] = ist_send[...]

    def tg_copy(h, b, k, slot):
        span = pl.ds(b * block, block)
        return head_copy(
            k, tg_part.at[h, span], tg_recv.at[slot, h, span],
            tg_s.at[h, b, k], tg_r.at[h, b, slot],
        )

    width = min(256, part_rows)

    def sum_heads(h, b):
        span = slice(b * block, (b + 1) * block)
        for c in range(lanes_half // width):
            part, start = c * width // part_rows, c * width % part_rows
            lanes = slice(h * lanes_half + c * width, h * lanes_half + (c + 1) * width)

            def add_owner(o, acc):
                weights = w_recv[h, o * split + part, :, start : start + width]
                for r in range(per_owner):
                    terms = probs[o * per_owner + r, span, lanes]
                    acc = acc + terms.astype(F32) * weights[r : r + 1]
                return acc

            tg_part[h, span, c * width : (c + 1) * width] = lax.fori_loop(
                0, n_ctx // split, add_owner, jnp.zeros((block, width), F32)
            )
        for k in range(1, n_head):
            tg_copy(h, b, k, my_head).start()

    recv_weights(0)
    for b in range(BLOCKS):
        sum_heads(0, b)
        if b == 0:
            send_weights(1)

    @pl.loop(1, n_ctx)
    def _(k):
        peer = peer_of(k, n_ctx, me)
        ist_copy(k, peer).wait_recv()

    itops = ist_recv[:, 0:1, :]
    imasses = ist_recv[:, 1:2, :]
    itop_all = jnp.max(itops, axis=0)
    itotal = jnp.sum(imasses * jnp.exp2(itops - itop_all[None]), axis=0)
    wi_ref[...] = jnp.exp2(ist_send[0:1, :] - itop_all) / itotal

    recv_weights(1)
    for b in range(BLOCKS):
        sum_heads(1, b)

    owners = n_ctx // 2
    for h in range(2):
        for b in range(BLOCKS):
            for k in range(1, n_head):
                tg_copy(h, b, k, peer_of(k, n_head, my_head)).wait_recv()
        lanes = slice(h * lanes_half, (h + 1) * lanes_half)
        target = tg_part[h]
        for k in range(1, n_head):
            target = target + tg_recv[peer_of(k, n_head, my_head), h]
        step = expo[:, lanes] * wi_ref[:, lanes] - target
        pst[:, lanes] = step
        ps_send[h * owners : (h + 1) * owners] = step.T.reshape(owners, own, keys)

        @pl.loop(0, owners)
        def _(k):
            peer = h * owners + lax.rem(me + k, owners)

            @pl.when(peer != me)
            def _():
                ps_copy(peer, me).start()

    ps_recv[me] = ps_send[me]

    kg_part[...] = jnp.zeros_like(kg_part)

    @pl.loop(0, iheads)
    def _(j):
        act = matmul_nt(ik_ref[...], iq_v[j])
        weight = hwt_ref[pl.ds(j, 1), :] * inv_scale
        terms = jnp.where(act > 0.0, pst[...] * weight, 0.0).astype(BF16)
        kg_part[...] += jnp.dot(terms, iq_v[j], preferred_element_type=F32)

    def kg_copy(k, slot):
        return head_copy(k, kg_part, kg_recv.at[slot], kg_s.at[k], kg_r.at[slot])

    for k in range(1, n_head):
        kg_copy(k, my_head).start()

    first = pl.multiple_of(me * own, own)
    for j in range(iheads):
        iqo[j * own : (j + 1) * own, :] = iq_v[j, pl.ds(first, own), :]
    qg[...] = jnp.zeros_like(qg)

    def add_source(source):
        source_keys = ikg[source].astype(BF16)
        act = matmul_nt(iqo[...], source_keys)
        terms = []
        for c in range(keys // 128):
            lanes = slice(c * 128, (c + 1) * 128)
            step = ps_recv[source, :, lanes]
            weighted = hwb[...].reshape(iheads, own, 128) * step[None]
            terms.append(
                jnp.where(act[:, lanes] > 0.0, weighted.reshape(iheads * own, 128), 0.0).astype(BF16)
            )
        qg[...] += jnp.dot(
            jnp.concatenate(terms, axis=1), source_keys, preferred_element_type=F32
        )

    for sub in range(2):
        ag_recv(sub, stages - 1)

    add_source(me)

    @pl.loop(1, n_ctx)
    def _(k):
        source = peer_of(k, n_ctx, me)
        ps_copy(source, source).wait_recv()
        add_source(source)

    for j in range(iheads):
        qgrad_ref[:, j * IDIM : (j + 1) * IDIM] = qg[j * own : (j + 1) * own, :]

    key_grad = kg_part[...]
    for k in range(1, n_head):
        slot = peer_of(k, n_head, my_head)
        kg_copy(k, slot).wait_recv()
        key_grad = key_grad + kg_recv[slot]
    kgrad_ref[...] = key_grad

    for s in range(stages):
        for sub in range(2):
            ag_sent(sub, s)
    for k in range(1, n_head):
        lg_copy(k, my_head).wait_send()
        kg_copy(k, my_head).wait_send()
        for h in range(2):
            for b in range(BLOCKS):
                tg_copy(h, b, k, my_head).wait_send()

    @pl.loop(1, n_ctx)
    def _(k):
        peer = peer_of(k, n_ctx, me)
        ist_copy(k, me).wait_send()
        for h in range(2):
            stat_copy(h, k, peer, me).wait_send()
            w_copy(h, k, peer, me).wait_send()
        ps_copy(peer, me).wait_send()


def shards(n_ctx, n_head, queries, attn_keys, index_queries, index_keys, head_weights, query_pos, key_offset):
    rows = queries.shape[0]
    keys = attn_keys.shape[0]
    heads = attn_keys.shape[1] // HEAD_DIM
    iheads = index_queries.shape[1] // IDIM
    own = rows // n_ctx
    pairs = heads // 2
    per_owner = max(1, heads // n_ctx)
    split = n_ctx * per_owner // heads
    stages = n_ctx.bit_length() - 1
    vmem = pltpu.VMEM
    dma = pltpu.SemaphoreType.DMA
    any_space = pl.BlockSpec(memory_space=pl.ANY)
    vmem_space = pl.BlockSpec(memory_space=pltpu.VMEM)
    return pl.pallas_call(
        functools.partial(kernel, n_ctx, n_head, heads),
        out_shape=(
            jax.ShapeDtypeStruct((own, iheads * IDIM), F32),
            jax.ShapeDtypeStruct((keys, IDIM), F32),
        ),
        in_specs=[any_space] * 3 + [vmem_space] * 4,
        out_specs=(vmem_space, vmem_space),
        scratch_shapes=[
            vmem((pairs, rows, 2 * HEAD_DIM), BF16),
            vmem((pairs, keys, 2 * HEAD_DIM), BF16),
            vmem((iheads, rows, IDIM), BF16),
            vmem((heads, keys, rows), BF16),
            vmem((n_ctx, keys, IDIM), F32),
            vmem((keys, rows), F32),
            vmem((keys, rows), F32),
            vmem((n_head, keys, rows), F32),
            vmem((keys, rows), F32),
            vmem((2, n_ctx, 2 * per_owner, rows // 2 // split), F32),
            vmem((2, n_ctx, 2 * per_owner, rows // 2 // split), F32),
            vmem((2, rows), F32),
            vmem((n_ctx, 2, rows), F32),
            vmem((2, n_ctx, per_owner, rows // 2 // split), F32),
            vmem((2, n_ctx, per_owner, rows // 2 // split), F32),
            vmem((1, rows), F32),
            vmem((2, keys, rows // 2), F32),
            vmem((n_head, 2, keys, rows // 2), F32),
            vmem((keys, rows), F32),
            vmem((n_ctx, own, keys), F32),
            vmem((n_ctx, own, keys), F32),
            vmem((keys, IDIM), F32),
            vmem((n_head, keys, IDIM), F32),
            vmem((iheads * own, IDIM), F32),
            vmem((iheads * own, 128), F32),
            vmem((rows, iheads), F32),
            vmem((iheads * own, IDIM), BF16),
            dma((pairs,)),
            dma((pairs,)),
            dma((iheads,)),
            dma((stages, 2, n_ctx)),
            dma((2, n_ctx)),
            dma((n_head,)),
            dma((n_head,)),
            dma((2, n_ctx)),
            dma((2, n_ctx)),
            dma((n_ctx,)),
            dma((n_ctx,)),
            dma((2, n_ctx)),
            dma((2, n_ctx)),
            dma((2, BLOCKS, n_head)),
            dma((2, BLOCKS, n_head)),
            dma((n_ctx,)),
            dma((n_ctx,)),
            dma((n_head,)),
            dma((n_head,)),
        ],
        compiler_params=pltpu.CompilerParams(
            collective_id=0, has_side_effects=True, vmem_limit_bytes=64 * 1024 * 1024 - 65536
        ),
    )(
        queries,
        attn_keys,
        index_queries,
        index_keys,
        head_weights.T,
        query_pos.reshape(1, rows),
        key_offset.reshape(1, keys),
    )


def solution(mesh):
    in_specs = (
        P(None, "head"),
        P("ctx", "head"),
        P(None, "head"),
        P("ctx", None),
        P(None, "head"),
        P(),
        P("ctx"),
    )
    out_specs = (P("ctx", "head"), P("ctx", None))
    body = functools.partial(shards, mesh.shape["ctx"], mesh.shape["head"])
    return jax.shard_map(body, mesh=mesh, in_specs=in_specs, out_specs=out_specs, check_vma=False)
```

time: 101 us -> 92.7 us (0.918)
  Pallas kernels: 93.1 us -> 88.4 us
  local copies, waits for them, and re-layouts: 7.04 us -> 3.44 us
    pallas_call x1, Pallas kernels: 93.1 us -> 88.4 us  [shards(): pl.pallas_call(functools.partial(kernel, n_ctx, n_head, heads), out_shape...]
    reshape x2 -> x0, local copies, waits for them, and re-layouts: 2.81 us -> none  [the longest x1 1.47 us: shards(): key_offset.reshape(keys, 1)]
where the time goes in v2:
time: 92.7 us; the launch traced here: 92.5 us
  Pallas kernels  88.4 us (95%)
  local copies, waits for them, and re-layouts  3.44 us (4%)
    pallas_call x1, Pallas kernels, shards(): pl.pallas_call(functools.partial(kernel, n_ctx, n_head, heads), out_shape...  88.4 us
    unnamed x2, local copies, waits for them, and re-layouts  3.44 us

profile of v2, /device:TPU:0, one launch (start us, length us, event | category | flops | bytes accessed | tf_op | source)
XLA Modules:
  0.0 92.5 jit_solution(17718731722524473410)
XLA Ops:
  0.6 88.4 %shard_map.86 = (f32[32,4096]{1,0:T(8,128)}, f32[256,128]{1,0:T(8,128)}) custom-call(bf16[512,12288]{1,0:T(8,128)(2,1)} %q_hbm.1, bf16[256,12288]{1,0:T(8,128)(2,1)} %k_hbm.1, bf16[512,4096]{1,0:T(8,128)(2,1)} %iq_hbm.1, bf16[256,128]{1,0:T(8,128)(2,1)} %ik_ref.1, f32[32,512]{1,0:T(8,128)} %bitcast.3, s32[1,512]{1,0:T(1,128)} %bitcast.4, s32[1,256]{1,0:T(1,128)} %bitcast.5), custom_call_target="tpu_custom_call" | custom-call | tf_op jit(solution)/shard_map/pallas_call | solution.py:444
  89.0 1.9 %copy.11 = f32[32,4096]{1,0:T(8,128)} copy(f32[32,4096]{1,0:T(8,128)} %get-tuple-element.4) | data formatting | bytes 1048576
  90.9 1.6 %copy.12 = f32[256,128]{1,0:T(8,128)} copy(f32[256,128]{1,0:T(8,128)} %get-tuple-element.5) | data formatting | bytes 262144

commit v3 on v2

--- a/solution.py
+++ b/solution.py
@@ -15,6 +15,8 @@
 NEG_FILL = -1e30
 LOG2E = math.log2(math.e)
 BLOCKS = 2
+GROUP = 4
+IQ_PARTS = 4
 MESH = pl.DeviceIdType.MESH
 F32 = jnp.float32
 BF16 = jnp.bfloat16
@@ -37,9 +39,13 @@
 ):
     me = lax.axis_index("ctx")
     my_head = lax.axis_index("head")
-    pairs, rows, pair_width = q_v.shape
+    groups, rows, group_width = q_v.shape
+    pair_width = 2 * HEAD_DIM
+    group = group_width // pair_width
+    pairs = groups * group
     keys = k_v.shape[1]
-    iheads = iq_v.shape[0]
+    iheads = iq_v.shape[1] // IDIM
+    iq_rows = rows // IQ_PARTS
     own = rows // n_ctx
     per_owner = max(1, 2 * pairs // n_ctx)
     split = n_ctx * per_owner // (2 * pairs)
@@ -53,22 +59,25 @@
         return lax.rem(base + k, n)
 
     def q_copy(p):
-        cols = pl.ds(pl.multiple_of(p * pair_width, 128), pair_width)
+        cols = pl.ds(pl.multiple_of(p * group_width, 128), group_width)
         return pltpu.make_async_copy(q_hbm.at[:, cols], q_v.at[p], q_sem.at[p])
 
     def k_copy(p):
-        cols = pl.ds(pl.multiple_of(p * pair_width, 128), pair_width)
+        cols = pl.ds(pl.multiple_of(p * group_width, 128), group_width)
         return pltpu.make_async_copy(k_hbm.at[:, cols], k_v.at[p], k_sem.at[p])
 
     def iq_copy(j):
-        cols = pl.ds(pl.multiple_of(j * IDIM, 128), IDIM)
-        return pltpu.make_async_copy(iq_hbm.at[:, cols], iq_v.at[j], iq_sem.at[j])
-
-    @pl.loop(0, iheads)
+        span = pl.ds(pl.multiple_of(j * iq_rows, iq_rows), iq_rows)
+        return pltpu.make_async_copy(iq_hbm.at[span], iq_v.at[span], iq_sem.at[j])
+
+    def iq_head(j):
+        return iq_v[:, pl.ds(pl.multiple_of(j * IDIM, 128), IDIM)]
+
+    @pl.loop(0, IQ_PARTS)
     def _(j):
         iq_copy(j).start()
 
-    @pl.loop(0, pairs)
+    @pl.loop(0, groups)
     def _(p):
         q_copy(p).start()
         k_copy(p).start()
@@ -138,10 +147,13 @@
     for sub in range(2):
         ag_start(sub, 0)
 
+    @pl.loop(0, IQ_PARTS)
+    def _(j):
+        iq_copy(j).wait()
+
     @pl.loop(0, iheads)
     def _(j):
-        iq_copy(j).wait()
-        act = matmul_nt(ik_ref[...], iq_v[j])
+        act = matmul_nt(ik_ref[...], iq_head(j))
         weight = hwt_ref[pl.ds(j, 1), :] * inv_scale
         lg_part[...] += weight * jnp.maximum(act, 0.0)
 
@@ -219,9 +231,10 @@
         span = slice(h * lanes_half, (h + 1) * lanes_half)
         for a in range(2):
             kept = column < HEAD_DIM if a == 0 else column >= 256 - HEAD_DIM
-            k_head = k_v[p, :, a * 128 : a * 128 + 256]
+            start = pl.multiple_of(lax.rem(p, group) * pair_width + a * 128, 128)
+            k_head = k_v[lax.div(p, group), :, pl.ds(start, 256)]
             k_head = jnp.where(kept, k_head, jnp.zeros_like(k_head))
-            scores = matmul_nt(k_head, q_v[p, span, a * 128 : a * 128 + 256])
+            scores = matmul_nt(k_head, q_v[lax.div(p, group), span, pl.ds(start, 256)])
             scores = scores * score_scale + bias[:, span]
             top = jnp.max(scores, axis=0, keepdims=True)
             expo_head = jnp.exp2(scores - top)
@@ -246,8 +259,12 @@
         @pl.loop(0, pairs)
         def _(p):
             if h == 0:
-                q_copy(p).wait()
-                k_copy(p).wait()
+
+                @pl.when(lax.rem(p, group) == 0)
+                def _():
+                    q_copy(lax.div(p, group)).wait()
+                    k_copy(lax.div(p, group)).wait()
+
             attn_pair(h, p)
             if h == 1:
                 pl.when(p == pairs // 2)(functools.partial(send_weights, 0))
@@ -355,10 +372,10 @@
 
     @pl.loop(0, iheads)
     def _(j):
-        act = matmul_nt(ik_ref[...], iq_v[j])
+        act = matmul_nt(ik_ref[...], iq_head(j))
         weight = hwt_ref[pl.ds(j, 1), :] * inv_scale
         terms = jnp.where(act > 0.0, pst[...] * weight, 0.0).astype(BF16)
-        kg_part[...] += jnp.dot(terms, iq_v[j], preferred_element_type=F32)
+        kg_part[...] += jnp.dot(terms, iq_head(j), preferred_element_type=F32)
 
     def kg_copy(k, slot):
         return head_copy(k, kg_part, kg_recv.at[slot], kg_s.at[k], kg_r.at[slot])
@@ -368,7 +385,7 @@
 
     first = pl.multiple_of(me * own, own)
     for j in range(iheads):
-        iqo[j * own : (j + 1) * own, :] = iq_v[j, pl.ds(first, own), :]
+        iqo[j * own : (j + 1) * own, :] = iq_v[pl.ds(first, own), j * IDIM : (j + 1) * IDIM]
     qg[...] = jnp.zeros_like(qg)
 
     def add_source(source):
@@ -433,7 +450,8 @@
     heads = attn_keys.shape[1] // HEAD_DIM
     iheads = index_queries.shape[1] // IDIM
     own = rows // n_ctx
-    pairs = heads // 2
+    group = math.gcd(GROUP, heads // 2)
+    groups = heads // 2 // group
     per_owner = max(1, heads // n_ctx)
     split = n_ctx * per_owner // heads
     stages = n_ctx.bit_length() - 1
@@ -450,9 +468,9 @@
         in_specs=[any_space] * 3 + [vmem_space] * 4,
         out_specs=(vmem_space, vmem_space),
         scratch_shapes=[
-            vmem((pairs, rows, 2 * HEAD_DIM), BF16),
-            vmem((pairs, keys, 2 * HEAD_DIM), BF16),
-            vmem((iheads, rows, IDIM), BF16),
+            vmem((groups, rows, 2 * HEAD_DIM * group), BF16),
+            vmem((groups, keys, 2 * HEAD_DIM * group), BF16),
+            vmem((rows, iheads * IDIM), BF16),
             vmem((heads, keys, rows), BF16),
             vmem((n_ctx, keys, IDIM), F32),
             vmem((keys, rows), F32),
@@ -477,9 +495,9 @@
             vmem((iheads * own, 128), F32),
             vmem((rows, iheads), F32),
             vmem((iheads * own, IDIM), BF16),
-            dma((pairs,)),
-            dma((pairs,)),
-            dma((iheads,)),
+            dma((groups,)),
+            dma((groups,)),
+            dma((IQ_PARTS,)),
             dma((stages, 2, n_ctx)),
             dma((2, n_ctx)),
             dma((n_head,)),

time: 92.7 us -> 91.9 us (level)
  no operation moved by 1% of the time
where the time goes in v3:
time: 91.9 us; the launch traced here: 91.6 us
  Pallas kernels  87.6 us (95%)
  local copies, waits for them, and re-layouts  3.44 us (4%)
    pallas_call x1, Pallas kernels, shards(): pl.pallas_call(functools.partial(kernel, n_ctx, n_head, heads), out_shape...  87.6 us
    unnamed x2, local copies, waits for them, and re-layouts  3.44 us

profile of v3, /device:TPU:0, one launch (start us, length us, event | category | flops | bytes accessed | tf_op | source)
XLA Modules:
  0.0 91.6 jit_solution(9177505687441900797)
XLA Ops:
  0.6 87.6 %shard_map.86 = (f32[32,4096]{1,0:T(8,128)}, f32[256,128]{1,0:T(8,128)}) custom-call(bf16[512,12288]{1,0:T(8,128)(2,1)} %q_hbm.1, bf16[256,12288]{1,0:T(8,128)(2,1)} %k_hbm.1, bf16[512,4096]{1,0:T(8,128)(2,1)} %iq_hbm.1, bf16[256,128]{1,0:T(8,128)(2,1)} %ik_ref.1, f32[32,512]{1,0:T(8,128)} %bitcast.3, s32[1,512]{1,0:T(1,128)} %bitcast.4, s32[1,256]{1,0:T(1,128)} %bitcast.5), custom_call_target="tpu_custom_call" | custom-call | tf_op jit(solution)/shard_map/pallas_call | solution.py:462
  88.2 1.9 %copy.11 = f32[32,4096]{1,0:T(8,128)} copy(f32[32,4096]{1,0:T(8,128)} %get-tuple-element.4) | data formatting | bytes 1048576
  90.1 1.6 %copy.12 = f32[256,128]{1,0:T(8,128)} copy(f32[256,128]{1,0:T(8,128)} %get-tuple-element.5) | data formatting | bytes 262144

commit v4 on v3

--- a/solution.py
+++ b/solution.py
@@ -151,7 +151,7 @@
     def _(j):
         iq_copy(j).wait()
 
-    @pl.loop(0, iheads)
+    @pl.loop(0, iheads, unroll=2)
     def _(j):
         act = matmul_nt(ik_ref[...], iq_head(j))
         weight = hwt_ref[pl.ds(j, 1), :] * inv_scale
@@ -319,7 +319,7 @@
                 return acc
 
             tg_part[h, span, c * width : (c + 1) * width] = lax.fori_loop(
-                0, n_ctx // split, add_owner, jnp.zeros((block, width), F32)
+                0, n_ctx // split, add_owner, jnp.zeros((block, width), F32), unroll=2
             )
         for k in range(1, n_head):
             tg_copy(h, b, k, my_head).start()
@@ -370,7 +370,7 @@
 
     kg_part[...] = jnp.zeros_like(kg_part)
 
-    @pl.loop(0, iheads)
+    @pl.loop(0, iheads, unroll=2)
     def _(j):
         act = matmul_nt(ik_ref[...], iq_head(j))
         weight = hwt_ref[pl.ds(j, 1), :] * inv_scale

time: 91.9 us -> 87.4 us (0.951)
  Pallas kernels: 87.6 us -> 83.1 us
    pallas_call x1, Pallas kernels: 87.6 us -> 83.1 us  [shards(): pl.pallas_call(functools.partial(kernel, n_ctx, n_head, heads), out_shape...]
where the time goes in v4:
time: 87.4 us; the launch traced here: 87.1 us
  Pallas kernels  83.1 us (95%)
  local copies, waits for them, and re-layouts  3.44 us (4%)
    pallas_call x1, Pallas kernels, shards(): pl.pallas_call(functools.partial(kernel, n_ctx, n_head, heads), out_shape...  83.1 us
    unnamed x2, local copies, waits for them, and re-layouts  3.44 us

profile of v4, /device:TPU:0, one launch (start us, length us, event | category | flops | bytes accessed | tf_op | source)
XLA Modules:
  0.0 87.1 jit_solution(2763654367549814872)
XLA Ops:
  0.6 83.1 %shard_map.86 = (f32[32,4096]{1,0:T(8,128)}, f32[256,128]{1,0:T(8,128)}) custom-call(bf16[512,12288]{1,0:T(8,128)(2,1)} %q_hbm.1, bf16[256,12288]{1,0:T(8,128)(2,1)} %k_hbm.1, bf16[512,4096]{1,0:T(8,128)(2,1)} %iq_hbm.1, bf16[256,128]{1,0:T(8,128)(2,1)} %ik_ref.1, f32[32,512]{1,0:T(8,128)} %bitcast.3, s32[1,512]{1,0:T(1,128)} %bitcast.4, s32[1,256]{1,0:T(1,128)} %bitcast.5), custom_call_target="tpu_custom_call" | custom-call | tf_op jit(solution)/shard_map/pallas_call | solution.py:462
  83.7 1.9 %copy.11 = f32[32,4096]{1,0:T(8,128)} copy(f32[32,4096]{1,0:T(8,128)} %get-tuple-element.4) | data formatting | bytes 1048576
  85.6 1.6 %copy.12 = f32[256,128]{1,0:T(8,128)} copy(f32[256,128]{1,0:T(8,128)} %get-tuple-element.5) | data formatting | bytes 262144
